TPU v7x, 128 devices: a whole 4x4x4 slice. The times are simulated.
128 devices in a mesh: dp: 16 (over z, x), tensor: 8 (over y, core).
Axes of the slice: x: 4, y: 4, z: 4, core: 2. Of those that a mesh axis runs over, the one named last changes fastest.
Arguments:
- tokens: bfloat16 [128, 128, 8192], P('dp', None, 'tensor'), may hold values from -6 to 6
- shared_prefix_tokens: bfloat16 [16, 256, 8192], P('dp', None, 'tensor'), may hold values from -6 to 6
- input_norm_gain: bfloat16 [8192], replicated, may hold values from 0.5 to 8
- query_weight: bfloat16 [8192, 8192], P(None, 'tensor'), may hold values from -0.0625 to 0.0625
- key_weight: bfloat16 [8192, 1024], P(None, 'tensor'), may hold values from -0.0625 to 0.0625
- value_weight: bfloat16 [8192, 1024], P(None, 'tensor'), may hold values from -0.0625 to 0.0625
- adapter_down_weight: bfloat16 [64, 8192, 16], P('dp', 'tensor'), may hold values from -0.0625 to 0.0625
- adapter_up_weight: bfloat16 [64, 16, 8192], P('dp', None, 'tensor'), may hold values from -0.75 to 0.75
- adapter_position: int32 [64], replicated, may hold values from 0 to 63, as said below
- request_adapter: int32 [128], P('dp'), may hold values from 0 to 63, as said below
- request_group: int32 [128], P('dp'), may hold values from 0 to 15
- lengths: int32 [128], P('dp'), may hold values from 1 to 128
- request_page_table: int32 [128, 1], P('dp'), may hold values from 0 to 127, as said below
Outputs:
- context: bfloat16 [128, 128, 8192], P('dp', None, 'tensor')
- paged_key_values: bfloat16 [128, 2, 128, 1024], P('dp', None, None, 'tensor')
Inputs may be any that keep to these rules, and one draw needn't show every extreme that they name: A permutation: adapter a is held at slot adapter_position[a], on index adapter_position[a] // 4 of dp. `request_adapter`: the 8 requests of one index of dp use adapters held by 8 different indices of dp. `request_page_table`: the requests of index i of dp use the pages i * 8 to (i + 1) * 8 - 1, each page once.
All inputs are finite; a program needn't handle non-finite values.
Results may differ from a plain program's by a relative error of at most 0.011.
The roundings to bfloat16 on the way count: a program that leaves them out, or rounds other values in their place, can miss the bound.
Values may be sent and summed in bfloat16 or wider, within the bound.
No kernel may reach another device: no remote copies, remote signals or barrier semaphores. Data moves between devices by JAX's collectives and lax.ppermute only.
A program may use at most 128 MiB of HBM per device.

v0:
```python
import jax
import jax.numpy as jnp
from jax import lax
from jax.sharding import PartitionSpec as P

HEAD_WIDTH = 128
ADAPTER_RANK = 16
PAGE_TOKENS = 128
EPS = 1e-05
THETA = 500000.0
ADAPTER_SCALE = 2.0


def rope_tables(positions, width):
    half = width // 2
    freq = THETA ** (-(jnp.arange(half, dtype=jnp.float32) * 2.0 / width))
    angle = positions.astype(jnp.float32)[:, None] * freq[None, :]
    return (jnp.cos(angle), jnp.sin(angle))


def apply_rope(values, cosine, sine):
    half = values.shape[-1] // 2
    first = values[..., :half]
    second = values[..., half:]
    cos_b = cosine[:, None, :]
    sin_b = sine[:, None, :]
    return jnp.concatenate(
        [first * cos_b - second * sin_b, second * cos_b + first * sin_b], axis=-1
    )


def normalize(rows, gain):
    values = rows.astype(jnp.float32)
    scale = lax.rsqrt(jnp.mean(values * values, axis=-1, keepdims=True) + EPS)
    return (values * scale * gain.astype(jnp.float32)).astype(jnp.bfloat16)


def on_device(
    tokens,
    shared_prefix_tokens,
    input_norm_gain,
    query_weight,
    key_weight,
    value_weight,
    adapter_down_weight,
    adapter_up_weight,
    adapter_position,
    request_adapter,
    request_group,
    lengths,
    request_page_table,
):
    req_dev, seq_len, d_part = tokens.shape
    grp_dev, pre_len, _ = shared_prefix_tokens.shape
    q_width = query_weight.shape[1]
    kv_width = key_weight.shape[1]
    q_heads = q_width // HEAD_WIDTH
    kv_local = kv_width // HEAD_WIDTH
    group_members = q_heads // kv_local
    token_rows = req_dev * seq_len
    column = lax.axis_index("tensor")
    place = lax.axis_index("dp")
    full_tokens, full_prefix = (
        lax.all_gather(tokens.reshape(token_rows, d_part), "tensor", axis=1, tiled=True),
        lax.all_gather(
            shared_prefix_tokens.reshape(grp_dev * pre_len, d_part), "tensor", axis=1, tiled=True
        ),
    )
    normed_input = normalize(full_tokens, input_norm_gain)
    prefix_normed = normalize(full_prefix, input_norm_gain)
    pre_cos, pre_sin = rope_tables(jnp.arange(pre_len), HEAD_WIDTH)
    pre_keys = jnp.dot(prefix_normed, key_weight, preferred_element_type=jnp.float32).reshape(
        grp_dev, pre_len, kv_local, HEAD_WIDTH
    )
    pre_keys = (
        apply_rope(pre_keys, pre_cos, pre_sin)
        .astype(jnp.bfloat16)
        .reshape(grp_dev, pre_len, kv_width)
    )
    pre_vals = (
        jnp.dot(prefix_normed, value_weight, preferred_element_type=jnp.float32)
        .astype(jnp.bfloat16)
        .reshape(grp_dev, pre_len, kv_width)
    )
    all_pairs = lax.all_gather(jnp.stack([pre_keys, pre_vals], 1), "dp", axis=0, tiled=True)
    table_ids = jnp.arange(adapter_position.shape[0])
    slots = jnp.sum(
        jnp.where(request_adapter[:, None] == table_ids[None, :], adapter_position[None, :], 0),
        axis=1,
    )
    local_rows = lax.dynamic_slice_in_dim(normed_input, column * d_part, d_part, 1)
    row_slot = jnp.repeat(slots, seq_len)
    page_piece = lax.all_gather(adapter_down_weight, "dp", axis=0, tiled=True)
    count = page_piece.shape[0]
    part = jnp.einsum("td,ndr->tnr", local_rows, page_piece, preferred_element_type=jnp.float32)
    pick = row_slot[:, None] == jnp.arange(count)[None, :]
    partial_low = jnp.sum(jnp.where(pick[:, :, None], part, 0.0), axis=1)
    low_rank_rows = lax.psum(partial_low, "tensor").astype(jnp.bfloat16)
    page_piece = lax.all_gather(adapter_up_weight, "dp", axis=0, tiled=True)
    count = page_piece.shape[0]
    pick = (row_slot[:, None] == jnp.arange(count)[None, :]).astype(jnp.bfloat16)
    spread = (pick[:, :, None] * low_rank_rows[:, None, :]).reshape(
        token_rows, count * ADAPTER_RANK
    )
    summed_rows = jnp.dot(
        spread,
        page_piece.reshape(count * ADAPTER_RANK, q_width),
        preferred_element_type=jnp.float32,
    )
    adapter_term = (ADAPTER_SCALE * summed_rows).astype(jnp.bfloat16)
    own_cos, own_sin = rope_tables(pre_len + jnp.arange(seq_len), HEAD_WIDTH)
    query_rows = jnp.dot(
        normed_input, query_weight, preferred_element_type=jnp.float32
    ) + adapter_term.astype(jnp.float32)
    query_rows = apply_rope(
        query_rows.reshape(req_dev, seq_len, q_heads, HEAD_WIDTH), own_cos, own_sin
    ).astype(jnp.bfloat16)
    key_rows = jnp.dot(normed_input, key_weight, preferred_element_type=jnp.float32).reshape(
        req_dev, seq_len, kv_local, HEAD_WIDTH
    )
    key_rows = apply_rope(key_rows, own_cos, own_sin).astype(jnp.bfloat16)
    value_rows = (
        jnp.dot(normed_input, value_weight, preferred_element_type=jnp.float32)
        .astype(jnp.bfloat16)
        .reshape(req_dev, seq_len, kv_local, HEAD_WIDTH)
    )
    live = jnp.arange(seq_len)[None, :] < lengths[:, None]
    key_rows = jnp.where(live[:, :, None, None], key_rows, jnp.zeros_like(key_rows))
    value_rows = jnp.where(live[:, :, None, None], value_rows, jnp.zeros_like(value_rows))
    chosen = all_pairs[request_group]
    all_keys = jnp.concatenate(
        [chosen[:, 0].reshape(req_dev, pre_len, kv_local, HEAD_WIDTH), key_rows], 1
    )
    all_vals = jnp.concatenate(
        [chosen[:, 1].reshape(req_dev, pre_len, kv_local, HEAD_WIDTH), value_rows], 1
    )
    grouped_query = query_rows.reshape(req_dev, seq_len, kv_local, group_members, HEAD_WIDTH)
    scores = jnp.einsum(
        "btkgd,bskd->bkgts", grouped_query, all_keys, preferred_element_type=jnp.float32
    ) * HEAD_WIDTH ** (-0.5)
    seen = jnp.arange(pre_len + seq_len)[None, :]
    allowed = (seen < pre_len) | (seen - pre_len <= jnp.arange(seq_len)[:, None])
    scores = jnp.where(allowed[None, None, None], scores, -1e30)
    top = jnp.max(scores, axis=-1, keepdims=True)
    weights = jnp.exp(scores - top)
    probs = (weights / jnp.sum(weights, axis=-1, keepdims=True)).astype(jnp.bfloat16)
    attention_output = jnp.einsum(
        "bkgts,bskd->btkgd", probs, all_vals, preferred_element_type=jnp.float32
    )
    attention_output = jnp.where(live[:, :, None, None, None], attention_output, 0.0)
    context = attention_output.reshape(req_dev, seq_len, q_width).astype(jnp.bfloat16)
    pages_req = seq_len // PAGE_TOKENS
    page_blocks = jnp.stack(
        [
            key_rows.reshape(req_dev, pages_req, PAGE_TOKENS, kv_width),
            value_rows.reshape(req_dev, pages_req, PAGE_TOKENS, kv_width),
        ],
        2,
    )
    page_blocks = page_blocks.reshape(req_dev * pages_req, 2, PAGE_TOKENS, kv_width)
    local_page = request_page_table.reshape(-1) - place * (req_dev * pages_req)
    paged_key_values = jnp.zeros_like(page_blocks).at[local_page].set(page_blocks)
    return (context, paged_key_values)


def solution(mesh):
    in_specs = (
        P("dp", None, "tensor"),
        P("dp", None, "tensor"),
        P(),
        P(None, "tensor"),
        P(None, "tensor"),
        P(None, "tensor"),
        P("dp", "tensor", None),
        P("dp", None, "tensor"),
        P(),
        P("dp"),
        P("dp"),
        P("dp"),
        P("dp", None),
    )
    out_specs = (P("dp", None, "tensor"), P("dp", None, None, "tensor"))
    return jax.shard_map(
        on_device, mesh=mesh, in_specs=in_specs, out_specs=out_specs, check_vma=False
    )
```

profile of v0, /device:TPU:0, one launch (start us, length us, event | category | flops | bytes accessed | tf_op | source)
XLA Modules:
  0.0 344.5 jit_solution(120121396503228455)
XLA Ops:
  8.0 0.7 convert_element_type.114
  8.7 35.6 %all-gather.15.cloned.1.call-done = bf16[1,256,8192]{2,1,0:T(8,128)(2,1)} async-done(((bf16[1,256,1024]{2,1,0:T(8,128)(2,1)}), bf16[1,256,8192]{2,1,0:T(8,128)(2,1)}) %all-gather.15.cloned.1.call-update) | async-done | bytes 4194320 | tf_op jit(solution)/shard_map/all_gather | solution.py:65
  44.3 3.3 fusion.5
  47.8 3.3 fusion.33
  51.5 1.7 fusion.39
  53.3 0.8 copy.63
  58.6 40.8 %all-gather.7.cloned.1.call-done = bf16[16,2,256,128]{3,2,1,0:T(8,128)(2,1)} async-done(((bf16[1,2,256,128]{3,2,1,0:T(8,128)(2,1)}), bf16[16,2,256,128]{3,2,1,0:T(8,128)(2,1)}) %all-gather.7.cloned.1.call-update) | async-done | bytes 2097168 | tf_op jit(solution)/shard_map/all_gather | solution.py:85
  99.4 2.5 gather_fusion
  101.9 1.0 fusion.67
  102.9 2.0 copy.78
  105.0 80.4 %all-gather.9.cloned.1.call-done = bf16[1024,8192]{1,0:T(8,128)(2,1)} async-done(((bf16[1024,1024]{1,0:T(8,128)(2,1)}), bf16[1024,8192]{1,0:T(8,128)(2,1)}) %all-gather.9.cloned.1.call-update) | async-done | bytes 16777232 | tf_op jit(solution)/shard_map/all_gather | solution.py:64
  185.4 7.5 %fusion = f32[1024]{0:T(1024)S(1)} fusion(bf16[1024,8192]{1,0:T(8,128)(2,1)} %all-gather.9.cloned.1.call-done), kind=kLoop, calls=%fused_computation.4 | loop fusion | flops 25164800 | bytes 16781312 | tf_op jit(solution)/shard_map/reduce_sum | solution.py:34
  192.9 3.2 copy-done.2
  196.0 8.3 %fusion.2 = bf16[1024,8192]{1,0:T(8,128)(2,1)} fusion(bf16[1024,8192]{1,0:T(8,128)(2,1)S(1)} %copy-done.2, f32[8192]{0:T(1024)S(1)} %convert_element_type.114, f32[1024]{0:T(1024)S(1)} %add_rsqrt_fusion), kind=kLoop, calls=%fused_computation.6 | loop fusion | flops 33554432 | bytes 33591296 | tf_op jit(solution)/shard_map/convert_element_type | solution.py:35
  204.3 29.0 %all-gather.11.cloned.1.call-done = bf16[64,1024,16]{1,2,0:T(8,128)(2,1)} async-done(((bf16[4,1024,16]{1,2,0:T(8,128)(2,1)}), bf16[64,1024,16]{1,2,0:T(8,128)(2,1)}) %all-gather.11.cloned.1.call-update) | async-done | bytes 2097168 | tf_op jit(solution)/shard_map/all_gather | solution.py:93
  233.3 5.1 %select_reduce_fusion = f32[1024,16]{0,1:T(8,128)S(1)} fusion(pred[1024,64]{0,1:T(8,128)(4,1)S(1)} %get-tuple-element.23, bf16[64,1024,16]{1,2,0:T(8,128)(2,1)} %all-gather.11.cloned.1.call-done, bf16[1024,8192]{1,0:T(8,128)(2,1)} %fusion.2, s32[]{:T(128)S(6)} %select_n.72), kind=kOutput, calls=%fused_computation.27 | convolution fusion | flops 2149564416 | bytes 4325380 | tf_op jit(solution)/shard_map/td,ndr->tnr/dot_general | solution.py:95
  238.4 25.3 %psum.7 = bf16[1024,16]{0,1:T(8,128)(2,1)S(1)} all-reduce(f32[1024,16]{0,1:T(8,128)S(1)} %select_reduce_fusion), channel_id=1, replica_groups=mesh['dp'=16,'tensor'=8] {'tensor'}, use_global_device_ids=true, to_apply=%region_4.5 | all-reduce | flops 16384 | bytes 98304 | tf_op jit(solution)/shard_map/psum | solution.py:98
  263.7 8.5 %convolution_convert_fusion = bf16[1024,128]{1,0:T(8,128)(2,1)S(1)} fusion(bf16[1024,8192]{1,0:T(8,128)(2,1)} %fusion.2, bf16[8192,128]{1,0:T(8,128)(2,1)S(1)} %copy-done), kind=kOutput, calls=%fused_computation.38 | convolution fusion | flops 2147614720 | bytes 19136512 | tf_op jit(solution)/shard_map/dot_general | solution.py:123
  272.2 2.4 copy-done.3
  275.2 4.5 %fusion.68 = f32[1024,128]{1,0:T(8,128)S(1)} fusion(bf16[1024,8192]{1,0:T(8,128)(2,1)S(1)} %copy-done.3, bf16[8192,128]{1,0:T(8,128)(2,1)S(1)} %copy-done.11), kind=kOutput, calls=%fused_computation.101 | convolution fusion | flops 2147483648 | bytes 19398656 | tf_op jit(solution)/shard_map/dot_general | solution.py:118
  279.8 5.4 %fusion.12 = bf16[1024,1024]{1,0:T(8,128)(2,1)S(1)} fusion(bf16[64,16,1024]{2,1,0:T(8,128)(2,1)} %all-gather.13.cloned.1.call-done, bf16[1024,16]{0,1:T(8,128)(2,1)S(1)} %psum.7, bf16[1024,64]{0,1:T(8,128)(2,1)S(1)} %get-tuple-element.22), kind=kOutput, calls=%fused_computation.23 | convolution fusion | flops 2150629376 | bytes 4358144 | tf_op jit(solution)/shard_map/dot_general | solution.py:105
  285.3 22.6 %add_bitcast_fusion = f32[128,8,8,128]{3,1,2,0:T(8,128)S(1)} fusion(bf16[1024,1024]{1,0:T(8,128)(2,1)S(1)} %fusion.12, bf16[1024,8192]{1,0:T(8,128)(2,1)} %fusion.2, bf16[8192,1024]{1,0:T(8,128)(2,1)} %param.16), kind=kOutput, calls=%fused_computation.26 | convolution fusion | flops 17181966336 | bytes 39845888 | tf_op jit(solution)/shard_map/dot_general | solution.py:112
  307.9 1.0 copy.82
  308.9 4.6 %fusion.66 = (f32[8,128,8,64]{3,2,1,0:T(8,128)}, f32[8,128,8,64]{3,2,1,0:T(8,128)}) fusion(f32[8,128,8,128]{3,2,1,0:T(8,128)S(1)} %bitcast.99), kind=kLoop, calls=%fused_computation.99 | loop fusion | bytes 8388608 | tf_op jit(solution)/shard_map/slice | solution.py:23
  314.0 0.8 copy.65
  314.9 5.2 %subtract_convert_fusion = (bf16[8,128,8,64]{3,1,2,0:T(8,128)(2,1)S(1)}, bf16[8,128,8,64]{3,1,2,0:T(8,128)(2,1)S(1)}) fusion(f32[8,128,8,64]{3,2,1,0:T(8,128)} %get-tuple-element.15, f32[8,128,8,64]{3,2,1,0:T(8,128)} %get-tuple-element.14, f32[128,64]{1,0:T(8,128)S(1)} %get-tuple-element.29, f32[128,64]{1,0:T(8,128)S(1)} %get-tuple-element.28), kind=kLoop, calls=%fused_computation.25 | loop fusion | flops 4194304 | bytes 6356992 | tf_op jit(solution)/shard_map/convert.4
  320.1 3.1 fusion.4
  323.2 3.2 fusion.3
  326.5 5.3 %fusion.11 = bf16[8,1,128,8,128]{4,2,3,0,1:T(8,128)(2,1)} fusion(f32[8,8,128]{2,1,0:T(8,128)S(1)} %fusion.3, f32[8,8,128]{2,1,0:T(8,128)S(1)} %get-tuple-element.30, f32[8,384,128,8]{2,1,3,0:T(8,128)S(1)} %get-tuple-element.31, pred[128,384]{0,1:T(8,128)(4,1)S(1)} %fusion.48, pred[8,128]{1,0:T(8,128)(4,1)S(1)} %copy-done.9, ...), kind=kOutput, calls=%fused_computation.21 | convolution fusion | flops 824705024 | bytes 15582208 | tf_op jit(solution)/shard_map/bkgts,bskd->btkgd/dot_general | solution.py:147
  331.7 4.1 %copy.73 = bf16[8,128,1024]{2,1,0:T(8,128)(2,1)} copy(bf16[8,128,1024]{1,2,0:T(8,128)(2,1)} %bitcast.103) | data formatting | bytes 4194304
  336.3 0.9 scatter_fusion
  337.2 0.8 copy-done.6
  (66 shorter events, 7.6 us)
Async XLA Ops:
  7.2 44.3 %copy-start = (bf16[8192,128]{1,0:T(8,128)(2,1)S(1)}, bf16[8192,128]{1,0:T(8,128)(2,1)}, u32[]{:S(2)}) copy-start(bf16[8192,128]{1,0:T(8,128)(2,1)} %param.18) | copy-start | bytes 6291460
  7.2 37.2 %all-gather.15.cloned.1.call-start = ((), (), s32[]{:S(2)}) async-start(), calls=%async_computation.4 | async-start | bytes 4718592 | tf_op jit(solution)/shard_map/all_gather | solution.py:65
  7.9 91.5 %all-gather.7.cloned.1.call-start = ((), (), s32[]{:S(2)}) async-start(), calls=%async_computation | async-start | bytes 2228224 | tf_op jit(solution)/shard_map/all_gather | solution.py:85
  44.3 3.4 %copy-start.4 = (bf16[1,256,8192]{2,1,0:T(8,128)(2,1)S(1)}, bf16[1,256,8192]{2,1,0:T(8,128)(2,1)}, u32[]{:S(2)}) copy-start(bf16[1,256,8192]{2,1,0:T(8,128)(2,1)} %all-gather.15.cloned.1.call-done) | copy-start | bytes 12582916
  51.5 4.6 %copy-start.12 = (s32[64]{0:T(128)S(1)}, s32[64]{0:T(128)}, u32[]{:S(2)}) copy-start(s32[64]{0:T(128)} %param.21) | copy-start | bytes 772
  51.5 4.6 %copy-start.13 = (s32[8]{0:T(128)S(1)}, s32[8]{0:T(128)}, u32[]{:S(2)}) copy-start(s32[8]{0:T(128)} %param.22) | copy-start | bytes 100
  51.5 5.2 %copy-start.14 = (s32[8]{0:T(128)S(1)}, s32[8]{0:T(128)}, u32[]{:S(2)}) copy-start(s32[8]{0:T(128)} %param.24) | copy-start | bytes 100
  51.5 5.8 %copy-start.15 = (s32[8]{0:T(128)S(1)}, s32[8]{0:T(128)}, u32[]{:S(2)}) copy-start(s32[8]{0:T(128)} %param.23) | copy-start | bytes 100
  51.5 6.6 %copy-start.16 = (s32[8,1]{0,1:T(1,128)S(1)}, s32[8,1]{0,1:T(1,128)}, u32[]{:S(2)}) copy-start(s32[8,1]{0,1:T(1,128)} %param.25) | copy-start | bytes 100
  54.1 131.3 %all-gather.9.cloned.1.call-start = ((), (), s32[]{:S(2)}) async-start(), calls=%async_computation.1 | async-start | bytes 18874368 | tf_op jit(solution)/shard_map/all_gather | solution.py:64
  54.8 178.5 %all-gather.11.cloned.1.call-start = ((), (), s32[]{:S(2)}) async-start(), calls=%async_computation.2 | async-start | bytes 2228224 | tf_op jit(solution)/shard_map/all_gather | solution.py:93
  55.4 224.4 %all-gather.13.cloned.1.call-start = ((), (), s32[]{:S(2)}) async-start(), calls=%async_computation.3 | async-start | bytes 2228224 | tf_op jit(solution)/shard_map/all_gather | solution.py:99
  185.4 10.7 %copy-start.2 = (bf16[1024,8192]{1,0:T(8,128)(2,1)S(1)}, bf16[1024,8192]{1,0:T(8,128)(2,1)}, u32[]{:S(2)}) copy-start(bf16[1024,8192]{1,0:T(8,128)(2,1)} %all-gather.9.cloned.1.call-done) | copy-start | bytes 50331652
  263.7 10.9 %copy-start.3 = (bf16[1024,8192]{1,0:T(8,128)(2,1)S(1)}, bf16[1024,8192]{1,0:T(8,128)(2,1)}, u32[]{:S(2)}) copy-start(bf16[1024,8192]{1,0:T(8,128)(2,1)} %fusion.2) | copy-start | bytes 50331652
  263.7 11.5 %copy-start.11 = (bf16[8192,128]{1,0:T(8,128)(2,1)S(1)}, bf16[8192,128]{1,0:T(8,128)(2,1)}, u32[]{:S(2)}) copy-start(bf16[8192,128]{1,0:T(8,128)(2,1)} %param.17) | copy-start | bytes 6291460
  308.9 4.8 %copy-start.9 = (pred[8,128]{1,0:T(8,128)(4,1)S(1)}, pred[8,128]{1,0:T(8,128)(4,1)}, u32[]{:S(2)}) copy-start(pred[8,128]{1,0:T(8,128)(4,1)} %iota_compare_fusion.3) | copy-start | bytes 3076
  314.9 5.2 %copy-start.5 = (bf16[8,256,1,128]{3,1,0,2:T(8,128)(2,1)S(1)}, bf16[8,256,1,128]{3,1,0,2:T(8,128)(2,1)}, u32[]{:S(2)}) copy-start(bf16[8,256,1,128]{3,1,0,2:T(8,128)(2,1)} %get-tuple-element.17) | copy-start | bytes 1572868
  323.2 3.2 copy-start.7
  323.2 3.2 copy-start.8
  331.7 4.6 %copy-start.10 = (s32[8]{0:T(128)S(1)}, s32[8]{0:T(128)}, u32[]{:S(2)}) copy-start(s32[8]{0:T(128)} %fusion.59) | copy-start | bytes 100
  331.7 6.2 %copy-start.1 = (bf16[8192,128]{1,0:T(8,128)(2,1)S(1)}, bf16[8192,128]{1,0:T(8,128)(2,1)}, u32[]{:S(2)}) copy-start(bf16[8192,128]{1,0:T(8,128)(2,1)} %param.18) | copy-start | bytes 6291460
  337.2 0.8 copy-start.6
Sparse Core Ops, SparseCore 0:
  9.7 34.5 all-gather.14
  54.2 45.1 all-gather.6
  101.1 84.1 all-gather.8
  187.4 45.8 all-gather.10
  235.3 44.5 all-gather.12
where the time goes:
time: 345 us
  waiting for transfers between devices  188 us (54%)
  matrix products  59.5 us (17%)
  other arithmetic  31.9 us (9%)
  blocking collectives  25.3 us (7%)
  local copies, waits for them, and re-layouts  25.1 us (7%)
  between operations  14.2 us (4%)
    all_gather x1, waiting for transfers between devices, on_device(): lax.all_gather(tokens.reshape(token_rows, d_part), 'tensor', axis=1, tile...  80.4 us
    all_gather x1, waiting for transfers between devices, on_device(): lax.all_gather(jnp.stack([pre_keys, pre_vals], 1), 'dp', axis=0, tiled=True)  40.8 us
    all_gather x1, waiting for transfers between devices, on_device(): lax.all_gather(shared_prefix_tokens.reshape(grp_dev * pre_len, d_part), '...  35.6 us
    all_gather x1, waiting for transfers between devices, on_device(): page_piece = lax.all_gather(adapter_down_weight, 'dp', axis=0, tiled=True)  29 us
    psum x1, blocking collectives, on_device(): low_rank_rows = lax.psum(partial_low, 'tensor').astype(jnp.bfloat16)  25.3 us
    dot_general x1, matrix products, on_device(): jnp.dot(normed_input, query_weight, preferred_element_type=jnp.float32)  22.6 us
    unnamed x37, local copies, waits for them, and re-layouts  14.3 us
    reduce_sum x2, other arithmetic, normalize(): scale = lax.rsqrt(jnp.mean(values * values, axis=-1, keepdims=True) + EPS)  10.7 us
  transfers between devices with their start and end apart: 5, of which 5 were waited for; matrix products, arithmetic and copies ran while one was open for 12% of the time, Pallas kernels for 0%

commit v1 on v0

--- a/solution.py
+++ b/solution.py
@@ -62,8 +62,17 @@
     place = lax.axis_index("dp")
     full_tokens, full_prefix = (
         lax.all_gather(tokens.reshape(token_rows, d_part), "tensor", axis=1, tiled=True),
-        lax.all_gather(
-            shared_prefix_tokens.reshape(grp_dev * pre_len, d_part), "tensor", axis=1, tiled=True
+        jnp.concatenate(
+            lax.all_to_all(
+                jnp.stack(
+                    [shared_prefix_tokens.reshape(grp_dev * pre_len, d_part)]
+                    * lax.axis_size("tensor")
+                ),
+                "tensor",
+                0,
+                0,
+            ),
+            axis=1,
         ),
     )
     normed_input = normalize(full_tokens, input_norm_gain)

time: 345 us -> 366 us (1.061)
  waiting for transfers between devices: 188 us -> 202 us
  starting transfers between devices: 0.19 us -> 4.84 us
    all_to_all x0 -> x1, waiting for transfers between devices: none -> 49.7 us  [on_device(): lax.all_to_all(jnp.stack([shared_prefix_tokens.reshape(grp_dev * pre_len,...]
    all_gather x1 -> x0, waiting for transfers between devices: 35.6 us -> none  [on_device(): lax.all_gather(shared_prefix_tokens.reshape(grp_dev * pre_len, d_part), '...]
    all_to_all x0 -> x1, starting transfers between devices: none -> 4.69 us  [on_device(): lax.all_to_all(jnp.stack([shared_prefix_tokens.reshape(grp_dev * pre_len,...]
    convert_element_type x2 -> x3, other arithmetic: 8.99 us -> 11.3 us  [normalize(): return (values * scale * gain.astype(jnp.float32)).astype(jnp.bfloat16)]
    unnamed x37 -> x39, local copies, waits for them, and re-layouts: 14.3 us -> 14.2 us
  transfers between devices with their start and end apart: 5 -> 5, of which waited for: 5 -> 5; matrix products, arithmetic and copies ran while one was open for 12% -> 11% of each run, Pallas kernels for 0% -> 0%
where the time goes in v1:
time: 366 us
  waiting for transfers between devices  202 us (55%)
  matrix products  56.5 us (15%)
  other arithmetic  34.2 us (9%)
  local copies, waits for them, and re-layouts  28.5 us (8%)
  blocking collectives  25.3 us (7%)
  between operations  14.2 us (4%)
  starting transfers between devices  4.84 us (1%)
    all_gather x1, waiting for transfers between devices, on_device(): lax.all_gather(tokens.reshape(token_rows, d_part), 'tensor', axis=1, tile...  80.4 us
    all_to_all x1, waiting for transfers between devices, on_device(): lax.all_to_all(jnp.stack([shared_prefix_tokens.reshape(grp_dev * pre_len,...  49.7 us
    all_gather x1, waiting for transfers between devices, on_device(): lax.all_gather(jnp.stack([pre_keys, pre_vals], 1), 'dp', axis=0, tiled=True)  41.1 us
    all_gather x1, waiting for transfers between devices, on_device(): page_piece = lax.all_gather(adapter_down_weight, 'dp', axis=0, tiled=True)  29.1 us
    psum x1, blocking collectives, on_device(): low_rank_rows = lax.psum(partial_low, 'tensor').astype(jnp.bfloat16)  25.3 us
    dot_general x1, matrix products, on_device(): jnp.dot(normed_input, query_weight, preferred_element_type=jnp.float32)  22.6 us
    unnamed x39, local copies, waits for them, and re-layouts  14.2 us
    convert_element_type x3, other arithmetic, normalize(): return (values * scale * gain.astype(jnp.float32)).astype(jnp.bfloat16)  11.3 us
  transfers between devices with their start and end apart: 5, of which 5 were waited for; matrix products, arithmetic and copies ran while one was open for 11% of the time, Pallas kernels for 0%

profile of v1, /device:TPU:0, one launch (start us, length us, event | category | flops | bytes accessed | tf_op | source)
XLA Modules:
  0.0 365.9 jit_solution(2727654377425663415)
XLA Ops:
  7.2 1.4 copy.65
  8.6 2.3 stack.9
  10.8 4.7 %all-to-all-start = ((bf16[8,256,1024]{1,2,0:T(8,128)(2,1)}), bf16[8,256,1024]{1,2,0:T(8,128)(2,1)}, u32[]{:S(2)}, u32[]{:S(2)}) async-start(bf16[8,256,1024]{1,2,0:T(8,128)(2,1)} %stack.9), calls=%async_computation | async-start | bytes 8388608 | tf_op jit(solution)/shard_map/all_to_all | solution.py:66
  15.6 49.7 %all-to-all-done = bf16[8,256,1024]{1,2,0:T(8,128)(2,1)} async-done(((bf16[8,256,1024]{1,2,0:T(8,128)(2,1)}), bf16[8,256,1024]{1,2,0:T(8,128)(2,1)}, u32[]{:S(2)}, u32[]{:S(2)}) %all-to-all-start) | async-done | bytes 4194336 | tf_op jit(solution)/shard_map/all_to_all | solution.py:66
  65.3 3.3 multiply_reduce_fusion
  68.6 3.0 fusion.6
  71.6 1.0 convolution_bitcast_fusion
  72.7 1.0 fusion.28
  79.6 41.1 %all-gather.5.cloned.1.call-done = bf16[16,2,256,128]{3,2,1,0:T(8,128)(2,1)} async-done(((bf16[1,2,256,128]{3,2,1,0:T(8,128)(2,1)}), bf16[16,2,256,128]{3,2,1,0:T(8,128)(2,1)}) %all-gather.5.cloned.1.call-update) | async-done | bytes 2097168 | tf_op jit(solution)/shard_map/all_gather | solution.py:94
  120.7 2.5 gather_fusion
  123.2 1.0 fusion.54
  124.2 2.0 copy.82
  126.2 80.4 %all-gather.7.cloned.1.call-done = bf16[1024,8192]{1,0:T(8,128)(2,1)} async-done(((bf16[1024,1024]{1,0:T(8,128)(2,1)}), bf16[1024,8192]{1,0:T(8,128)(2,1)}) %all-gather.7.cloned.1.call-update) | async-done | bytes 16777232 | tf_op jit(solution)/shard_map/all_gather | solution.py:64
  206.6 7.5 %fusion = f32[1024]{0:T(1024)S(1)} fusion(bf16[1024,8192]{1,0:T(8,128)(2,1)} %all-gather.7.cloned.1.call-done), kind=kLoop, calls=%fused_computation.4 | loop fusion | flops 25164800 | bytes 16781312 | tf_op jit(solution)/shard_map/reduce_sum | solution.py:34
  214.1 3.2 copy-done.2
  217.3 8.3 %fusion.2 = bf16[1024,8192]{1,0:T(8,128)(2,1)} fusion(bf16[1024,8192]{1,0:T(8,128)(2,1)S(1)} %copy-done.2, f32[8192]{0:T(1024)S(1)} %convert_element_type.127, f32[1024]{0:T(1024)S(1)} %add_rsqrt_fusion), kind=kLoop, calls=%fused_computation.6 | loop fusion | flops 33554432 | bytes 33591296 | tf_op jit(solution)/shard_map/convert_element_type | solution.py:35
  225.5 29.1 %all-gather.9.cloned.1.call-done = bf16[64,1024,16]{1,2,0:T(8,128)(2,1)} async-done(((bf16[4,1024,16]{1,2,0:T(8,128)(2,1)}), bf16[64,1024,16]{1,2,0:T(8,128)(2,1)}) %all-gather.9.cloned.1.call-update) | async-done | bytes 2097168 | tf_op jit(solution)/shard_map/all_gather | solution.py:102
  254.7 5.1 %select_reduce_fusion = f32[1024,16]{0,1:T(8,128)S(1)} fusion(pred[1024,64]{0,1:T(8,128)(4,1)S(1)} %get-tuple-element.23, bf16[64,1024,16]{1,2,0:T(8,128)(2,1)} %all-gather.9.cloned.1.call-done, bf16[1024,8192]{1,0:T(8,128)(2,1)} %fusion.2, s32[]{:T(128)S(6)} %select_n.72), kind=kOutput, calls=%fused_computation.26 | convolution fusion | flops 2149564416 | bytes 4325380 | tf_op jit(solution)/shard_map/td,ndr->tnr/dot_general | solution.py:104
  259.8 25.3 %psum.7 = bf16[1024,16]{0,1:T(8,128)(2,1)S(1)} all-reduce(f32[1024,16]{0,1:T(8,128)S(1)} %select_reduce_fusion), channel_id=1, replica_groups=mesh['dp'=16,'tensor'=8] {'tensor'}, use_global_device_ids=true, to_apply=%region_4.5 | all-reduce | flops 16384 | bytes 98304 | tf_op jit(solution)/shard_map/psum | solution.py:107
  285.1 8.5 %convolution_convert_fusion = bf16[1024,128]{1,0:T(8,128)(2,1)S(1)} fusion(bf16[1024,8192]{1,0:T(8,128)(2,1)} %fusion.2, bf16[8192,128]{1,0:T(8,128)(2,1)S(1)} %copy-done), kind=kOutput, calls=%fused_computation.37 | convolution fusion | flops 2147614720 | bytes 19136512 | tf_op jit(solution)/shard_map/dot_general | solution.py:132
  293.6 2.4 copy-done.3
  296.6 4.5 %fusion.55 = f32[1024,128]{1,0:T(8,128)S(1)} fusion(bf16[1024,8192]{1,0:T(8,128)(2,1)S(1)} %copy-done.3, bf16[8192,128]{1,0:T(8,128)(2,1)S(1)} %copy-done.12), kind=kOutput, calls=%fused_computation.98 | convolution fusion | flops 2147483648 | bytes 19398656 | tf_op jit(solution)/shard_map/dot_general | solution.py:127
  301.2 5.4 %fusion.11 = bf16[1024,1024]{1,0:T(8,128)(2,1)S(1)} fusion(bf16[64,16,1024]{2,1,0:T(8,128)(2,1)} %all-gather.11.cloned.1.call-done, bf16[1024,16]{0,1:T(8,128)(2,1)S(1)} %psum.7, bf16[1024,64]{0,1:T(8,128)(2,1)S(1)} %get-tuple-element.22), kind=kOutput, calls=%fused_computation.22 | convolution fusion | flops 2150629376 | bytes 4358144 | tf_op jit(solution)/shard_map/dot_general | solution.py:114
  306.7 22.6 %add_bitcast_fusion = f32[128,8,8,128]{3,1,2,0:T(8,128)S(1)} fusion(bf16[1024,1024]{1,0:T(8,128)(2,1)S(1)} %fusion.11, bf16[1024,8192]{1,0:T(8,128)(2,1)} %fusion.2, bf16[8192,1024]{1,0:T(8,128)(2,1)} %param.16), kind=kOutput, calls=%fused_computation.25 | convolution fusion | flops 17181966336 | bytes 39845888 | tf_op jit(solution)/shard_map/dot_general | solution.py:121
  329.2 1.0 copy.86
  330.2 4.6 %fusion.53 = (f32[8,128,8,64]{3,2,1,0:T(8,128)}, f32[8,128,8,64]{3,2,1,0:T(8,128)}) fusion(f32[8,128,8,128]{3,2,1,0:T(8,128)S(1)} %bitcast.98), kind=kLoop, calls=%fused_computation.96 | loop fusion | bytes 8388608 | tf_op jit(solution)/shard_map/slice | solution.py:23
  336.2 5.2 %subtract_convert_fusion = (bf16[8,128,8,64]{3,1,2,0:T(8,128)(2,1)S(1)}, bf16[8,128,8,64]{3,1,2,0:T(8,128)(2,1)S(1)}) fusion(f32[8,128,8,64]{3,2,1,0:T(8,128)} %get-tuple-element.15, f32[8,128,8,64]{3,2,1,0:T(8,128)} %get-tuple-element.14, f32[128,64]{1,0:T(8,128)S(1)} %get-tuple-element.29, f32[128,64]{1,0:T(8,128)S(1)} %get-tuple-element.28), kind=kLoop, calls=%fused_computation.24 | loop fusion | flops 4194304 | bytes 6356992 | tf_op jit(solution)/shard_map/convert.6
  341.5 3.1 fusion.4
  344.6 3.2 fusion.3
  347.8 5.3 %fusion.10 = bf16[8,1,128,8,128]{4,2,3,0,1:T(8,128)(2,1)} fusion(f32[8,8,128]{2,1,0:T(8,128)S(1)} %fusion.3, f32[8,8,128]{2,1,0:T(8,128)S(1)} %get-tuple-element.30, f32[8,384,128,8]{2,1,3,0:T(8,128)S(1)} %get-tuple-element.31, pred[128,384]{0,1:T(8,128)(4,1)S(1)} %fusion.35, pred[8,128]{1,0:T(8,128)(4,1)S(1)} %copy-done.9, ...), kind=kOutput, calls=%fused_computation.20 | convolution fusion | flops 824705024 | bytes 15582208 | tf_op jit(solution)/shard_map/bkgts,bskd->btkgd/dot_general | solution.py:156
  353.1 4.1 %copy.77 = bf16[8,128,1024]{2,1,0:T(8,128)(2,1)} copy(bf16[8,128,1024]{1,2,0:T(8,128)(2,1)} %bitcast.102) | data formatting | bytes 4194304
  357.7 0.9 scatter_fusion
  (70 shorter events, 9.3 us)
Async XLA Ops:
  7.2 65.5 %copy-start = (bf16[8192,128]{1,0:T(8,128)(2,1)S(1)}, bf16[8192,128]{1,0:T(8,128)(2,1)}, u32[]{:S(2)}) copy-start(bf16[8192,128]{1,0:T(8,128)(2,1)} %param.18) | copy-start | bytes 6291460
  10.8 4.7 %copy-start.8 = (bf16[8192]{0:T(1024)(128)(2,1)S(1)}, bf16[8192]{0:T(1024)(128)(2,1)}, u32[]{:S(2)}) copy-start(bf16[8192]{0:T(1024)(128)(2,1)} %param.15) | copy-start | bytes 49156
  10.8 54.5 %all-to-all-start = ((bf16[8,256,1024]{1,2,0:T(8,128)(2,1)}), bf16[8,256,1024]{1,2,0:T(8,128)(2,1)}, u32[]{:S(2)}, u32[]{:S(2)}) async-start(bf16[8,256,1024]{1,2,0:T(8,128)(2,1)} %stack.9), calls=%async_computation | async-start | bytes 8388608 | tf_op jit(solution)/shard_map/all_to_all | solution.py:66
  15.5 105.2 %all-gather.5.cloned.1.call-start = ((), (), s32[]{:S(2)}) async-start(), calls=%async_computation.1 | async-start | bytes 2228224 | tf_op jit(solution)/shard_map/all_gather | solution.py:94
  68.6 3.0 copy-start.11
  72.7 4.3 %copy-start.13 = (s32[64]{0:T(128)S(1)}, s32[64]{0:T(128)}, u32[]{:S(2)}) copy-start(s32[64]{0:T(128)} %param.21) | copy-start | bytes 772
  72.7 4.3 %copy-start.14 = (s32[8]{0:T(128)S(1)}, s32[8]{0:T(128)}, u32[]{:S(2)}) copy-start(s32[8]{0:T(128)} %param.22) | copy-start | bytes 100
  72.7 5.0 %copy-start.15 = (s32[8]{0:T(128)S(1)}, s32[8]{0:T(128)}, u32[]{:S(2)}) copy-start(s32[8]{0:T(128)} %param.24) | copy-start | bytes 100
  72.7 5.6 %copy-start.16 = (s32[8]{0:T(128)S(1)}, s32[8]{0:T(128)}, u32[]{:S(2)}) copy-start(s32[8]{0:T(128)} %param.23) | copy-start | bytes 100
  72.7 6.4 %copy-start.17 = (s32[8,1]{0,1:T(1,128)S(1)}, s32[8,1]{0,1:T(1,128)}, u32[]{:S(2)}) copy-start(s32[8,1]{0,1:T(1,128)} %param.25) | copy-start | bytes 100
  74.9 131.7 %all-gather.7.cloned.1.call-start = ((), (), s32[]{:S(2)}) async-start(), calls=%async_computation.2 | async-start | bytes 18874368 | tf_op jit(solution)/shard_map/all_gather | solution.py:64
  75.7 179.0 %all-gather.9.cloned.1.call-start = ((), (), s32[]{:S(2)}) async-start(), calls=%async_computation.3 | async-start | bytes 2228224 | tf_op jit(solution)/shard_map/all_gather | solution.py:102
  76.4 224.8 %all-gather.11.cloned.1.call-start = ((), (), s32[]{:S(2)}) async-start(), calls=%async_computation.4 | async-start | bytes 2228224 | tf_op jit(solution)/shard_map/all_gather | solution.py:108
  206.6 10.7 %copy-start.2 = (bf16[1024,8192]{1,0:T(8,128)(2,1)S(1)}, bf16[1024,8192]{1,0:T(8,128)(2,1)}, u32[]{:S(2)}) copy-start(bf16[1024,8192]{1,0:T(8,128)(2,1)} %all-gather.7.cloned.1.call-done) | copy-start | bytes 50331652
  285.1 10.9 %copy-start.3 = (bf16[1024,8192]{1,0:T(8,128)(2,1)S(1)}, bf16[1024,8192]{1,0:T(8,128)(2,1)}, u32[]{:S(2)}) copy-start(bf16[1024,8192]{1,0:T(8,128)(2,1)} %fusion.2) | copy-start | bytes 50331652
  285.1 11.5 %copy-start.12 = (bf16[8192,128]{1,0:T(8,128)(2,1)S(1)}, bf16[8192,128]{1,0:T(8,128)(2,1)}, u32[]{:S(2)}) copy-start(bf16[8192,128]{1,0:T(8,128)(2,1)} %param.17) | copy-start | bytes 6291460
  330.2 4.8 %copy-start.9 = (pred[8,128]{1,0:T(8,128)(4,1)S(1)}, pred[8,128]{1,0:T(8,128)(4,1)}, u32[]{:S(2)}) copy-start(pred[8,128]{1,0:T(8,128)(4,1)} %iota_compare_fusion.3) | copy-start | bytes 3076
  336.2 5.2 %copy-start.4 = (bf16[8,256,1,128]{3,1,0,2:T(8,128)(2,1)S(1)}, bf16[8,256,1,128]{3,1,0,2:T(8,128)(2,1)}, u32[]{:S(2)}) copy-start(bf16[8,256,1,128]{3,1,0,2:T(8,128)(2,1)} %get-tuple-element.17) | copy-start | bytes 1572868
  344.6 3.2 copy-start.6
  344.6 3.2 copy-start.7
  353.1 4.6 %copy-start.10 = (s32[8]{0:T(128)S(1)}, s32[8]{0:T(128)}, u32[]{:S(2)}) copy-start(s32[8]{0:T(128)} %fusion.46) | copy-start | bytes 100
  353.1 6.2 %copy-start.1 = (bf16[8192,128]{1,0:T(8,128)(2,1)S(1)}, bf16[8192,128]{1,0:T(8,128)(2,1)}, u32[]{:S(2)}) copy-start(bf16[8192,128]{1,0:T(8,128)(2,1)} %param.18) | copy-start | bytes 6291460
  358.5 0.8 copy-start.5
Sparse Core Ops, SparseCore 0:
  75.0 45.6 all-gather.4
  122.4 84.1 all-gather.6
  208.8 45.8 all-gather.8
  256.7 44.5 all-gather.10
